TPU v7x, 32 devices: a whole 2x2x4 slice. The times are simulated.
32 devices in a mesh: seg: 4 (over z), blk: 8 (over y, x, core).
Axes of the slice: x: 2, y: 2, z: 4, core: 2. Of those that a mesh axis runs over, the one named last changes fastest.
Arguments:
- train_acts: bfloat16 [4, 1024, 512], P('seg', 'blk'), may hold values from -6 to 6
- train_grads: bfloat16 [4, 1024, 4096], P('seg', 'blk'), may hold values from -0.0059814453 to 0.0059814453
- counts: int32 [8], replicated, may hold values from 1 to 2, as said below
- basis_in: bfloat16 [4, 1, 512, 512], P('seg'), may hold values from -1 to 1, as said below
- basis_out: bfloat16 [4, 8, 512, 512], P('seg', 'blk'), may hold values from -1 to 1, as said below
- eigenvalues: bfloat16 [4, 8, 512, 512], P('seg', 'blk'), may hold values from 0.049804688 to 5
- back_weight: bfloat16 [4, 8, 512, 512], P('seg', 'blk'), may hold values from -0.25 to 0.25
- derivative: bfloat16 [4, 4, 32, 4096], P('seg', None, None, 'blk'), may hold values from 0 to 1
- query_acts: bfloat16 [4, 4, 32, 512], P('seg'), may hold values from -6 to 6
- query_top: bfloat16 [4, 32, 4096], P(None, None, 'blk'), may hold values from -0.0059814453 to 0.0059814453
Outputs:
- scores: float32 [4, 16], P(None, 'blk')
Inputs may be any that keep to these rules, and one draw needn't show every extreme that they name: In each pair of indices 2k and 2k+1 of blk one count is 2 and the other 1, so all counts add up to 12; slots below a device's count are valid. `basis_in`: each 512 x 512 matrix is orthogonal up to rounding. `basis_out`: each 512 x 512 matrix is orthogonal up to rounding.
All inputs are finite; a program needn't handle non-finite values.
Results may differ from a plain program's by a relative error of at most 0.015.
Values may be sent and summed in bfloat16 or wider, within the bound.
A program may use at most 64 MiB of HBM per device.

v0:
```python
import math
import jax
import jax.numpy as jnp
from jax import lax
from jax.sharding import PartitionSpec as P

TB = 64
SLOTS = 2
damping = 0.05


def passed_along(value, axis, steps):
    count = lax.axis_size(axis)
    first, last = (max(0, -steps), min(count, count - steps))
    return lax.ppermute(value, axis, [(source, source + steps) for source in range(first, last)])


def advance(current, weight, derivs):
    queries, query_tok, blk_width = current.shape
    mixed = jnp.dot(
        current.reshape(queries * query_tok, blk_width), weight, preferred_element_type=jnp.float32
    )
    mixed = mixed.reshape(queries, query_tok, blk_width)
    return (current.astype(jnp.float32) + mixed * derivs.astype(jnp.float32)).astype(jnp.bfloat16)


def precondition(current, acts_seg, inner_basis, outer_basis, eigen_block):
    queries, query_tok, blk_width = current.shape
    in_slices = inner_basis.shape[0]
    in_width = in_slices * blk_width
    rot_err = jnp.dot(
        current.reshape(queries * query_tok, blk_width),
        outer_basis,
        preferred_element_type=jnp.float32,
    )
    rot_err = rot_err.astype(jnp.bfloat16).reshape(queries, query_tok, blk_width)
    act_split = acts_seg.reshape(queries, query_tok, in_slices, blk_width)
    rot_acts = jnp.einsum(
        "qtid,ide->qtie", act_split, inner_basis, preferred_element_type=jnp.float32
    ).astype(jnp.bfloat16)
    core_raw = jnp.einsum("qtd,qtie->qdie", rot_err, rot_acts, preferred_element_type=jnp.float32)
    core_raw = core_raw.reshape(queries, blk_width, in_width)
    scaled_core = (core_raw / (eigen_block.astype(jnp.float32)[None] + damping)).astype(
        jnp.bfloat16
    )
    left_prod = jnp.einsum(
        "cd,qdf->qcf", outer_basis, scaled_core, preferred_element_type=jnp.float32
    ).astype(jnp.bfloat16)
    left_split = left_prod.reshape(queries, blk_width, in_slices, blk_width)
    precond = jnp.einsum(
        "qcie,ife->qcif", left_split, inner_basis, preferred_element_type=jnp.float32
    )
    return precond.astype(jnp.bfloat16).reshape(queries, blk_width, in_width)


def block_scores(grad_rows, act_rows, precond, slot_tokens):
    row_count = grad_rows.shape[0]
    group_count = max(row_count // slot_tokens, 1)
    group_rows = row_count // group_count
    batch_groups = math.gcd(group_count, 8)
    grad_groups = grad_rows.reshape(
        group_count // batch_groups, batch_groups, group_rows, grad_rows.shape[1]
    )
    act_groups = act_rows.reshape(
        group_count // batch_groups, batch_groups, group_rows, act_rows.shape[1]
    )

    def one_batch(operands):
        grad_block, act_block = operands
        outer_prod = jnp.einsum(
            "btd,bte->bde", grad_block, act_block, preferred_element_type=jnp.float32
        ).astype(jnp.bfloat16)
        return jnp.einsum("bde,qde->bq", outer_prod, precond, preferred_element_type=jnp.float32)

    partial_scores = lax.map(one_batch, (grad_groups, act_groups))
    return (partial_scores.reshape(group_count, precond.shape[0]), group_rows)


def body(
    train_acts,
    train_grads,
    counts,
    basis_in,
    basis_out,
    eigenvalues,
    back_weight,
    derivative,
    query_acts,
    query_top,
):
    seg_count = lax.axis_size("seg")
    seg_index = lax.axis_index("seg")
    blk_index = lax.axis_index("blk")
    n_slot = lax.axis_size("blk") * SLOTS
    slot_ids = jnp.arange(n_slot, dtype=jnp.int32)
    current = query_top
    for relay_step in range(seg_count - 1):
        moved = advance(current, back_weight[0, 0], derivative[0])
        arrived = passed_along(moved, "seg", -1)
        current = jnp.where(seg_index == seg_count - 2 - relay_step, arrived, current)
    precond = precondition(current, query_acts[0], basis_in[0], basis_out[0, 0], eigenvalues[0, 0])
    exchanged = lax.all_to_all(train_grads, "blk", split_axis=2, concat_axis=1, tiled=True)
    grad_rows = exchanged[0]
    scores_part, group_rows = block_scores(
        grad_rows, lax.all_gather(train_acts, "blk", axis=1, tiled=True)[0], precond, TB
    )
    slot_of = jnp.arange(scores_part.shape[0], dtype=jnp.int32) * group_rows // TB
    placement = (slot_of[:, None] == slot_ids[None, :]).astype(jnp.float32)
    local_scores = jnp.dot(scores_part.T, placement, precision=lax.Precision.HIGHEST)
    mine = lax.psum_scatter(local_scores, "blk", scatter_dimension=1, tiled=True)
    mine = lax.psum(mine, "seg")
    own_valid = (jnp.arange(SLOTS, dtype=jnp.int32) < counts[blk_index]).astype(jnp.float32)
    return mine * own_valid[None, :]


def solution(mesh):
    in_specs = (
        P("seg", "blk", None),
        P("seg", "blk", None),
        P(),
        P("seg", None, None, None),
        P("seg", "blk", None, None),
        P("seg", "blk", None, None),
        P("seg", "blk", None, None),
        P("seg", None, None, "blk"),
        P("seg", None, None, None),
        P(None, None, "blk"),
    )
    out_specs = P(None, "blk")
    return jax.shard_map(body, mesh=mesh, in_specs=in_specs, out_specs=out_specs, check_vma=False)
```

profile of v0, /device:TPU:0, one launch (start us, length us, event | category | flops | bytes accessed | tf_op | source)
XLA Modules:
  0.0 125.0 jit_solution(6837176893961638313)
XLA Ops:
  6.5 0.0 copy-start
  6.5 1.4 %fusion.15 = bf16[4,32,512]{2,1,0:T(8,128)(2,1)S(1)} fusion(bf16[4,32,512]{2,1,0:T(8,128)(2,1)} %param.21, bf16[1,1,512,512]{3,2,1,0:T(8,128)(2,1)} %param.18, bf16[1,4,32,512]{3,2,1,0:T(8,128)(2,1)} %param.19), kind=kOutput, calls=%fused_computation.20 | convolution fusion | flops 67436544 | bytes 917504 | tf_op jit(solution)/shard_map/dot_general | solution.py:20
  8.0 1.3 %collective-permute-start = (bf16[4,32,512]{2,1,0:T(8,128)(2,1)S(1)}, bf16[4,32,512]{2,1,0:T(8,128)(2,1)S(1)}, u32[]{:S(2)}, u32[]{:S(2)}) collective-permute-start(bf16[4,32,512]{2,1,0:T(8,128)(2,1)S(1)} %fusion.15), channel_id=1, source_target_pairs={{8,0},{16,8},{24,16},{9,1},{17,9},{25,17},{10,2},{18,10},{26,18},{... | collective-permute-start | bytes 393224 | tf_op jit(solution)/shard_map/ppermute | solution.py:15
  9.3 5.0 %copy.25 = bf16[1,128,4096]{1,0,2:T(2,128)(2,1)S(1)} copy(bf16[1,128,4096]{2,1,0:T(8,128)(2,1)} %param.13) | data formatting | bytes 2097152 | tf_op args[1]
  14.3 0.5 broadcast.63
  14.8 23.4 %reduce = bf16[4096,128]{1,0:T(8,128)(2,1)} reduce(bf16[4096,1,128]{2,1,0:T(2,128)(2,1)S(1)} %bitcast.92, bf16[]{:T(256)} %broadcast.63), dimensions={1}, to_apply=%bitcast.73.reduce_sub_computation | reduce | bytes 2097154
  38.2 2.2 %reshape.95 = bf16[8,2,32768]{2,1,0:T(2,128)(2,1)} reshape(bf16[4096,128]{1,0:T(8,128)(2,1)} %reduce) | data formatting | bytes 2097152
  40.4 5.3 %all-to-all-start = ((bf16[8,2,32768]{2,1,0:T(2,128)(2,1)}), bf16[8,2,32768]{2,1,0:T(2,128)(2,1)}, u32[]{:S(2)}, u32[]{:S(2)}) async-start(bf16[8,2,32768]{2,1,0:T(2,128)(2,1)} %reshape.95), calls=%async_computation | async-start | bytes 2097152 | tf_op jit(solution)/shard_map/all_to_all | solution.py:102
  45.8 0.0 all-gather.2.cloned.1.call-start
  45.8 0.7 all-gather.2.cloned.1.call-update
  46.5 0.0 collective-permute-done
  46.5 0.0 copy-done.5
  46.6 0.0 copy-done.1
  46.6 0.0 copy-start.9
  46.6 0.0 copy-start.8
  46.6 0.2 add_convert_fusion.1
  46.9 1.3 %collective-permute-start.1 = (bf16[4,32,512]{2,1,0:T(8,128)(2,1)S(1)}, bf16[4,32,512]{2,1,0:T(8,128)(2,1)S(1)}, u32[]{:S(2)}, u32[]{:S(2)}) collective-permute-start(bf16[4,32,512]{2,1,0:T(8,128)(2,1)S(1)} %add_convert_fusion.1), channel_id=1, source_target_pairs={{8,0},{16,8},{24,16},{9,1},{17,9},{25,17},{10,2},{18,10},{26,18},{... | collective-permute-start | bytes 393224 | tf_op jit(solution)/shard_map/ppermute | solution.py:15
  48.2 0.0 copy-done.3
  48.2 0.1 add_bitcast_fusion
  48.3 7.2 %collective-permute-done.1 = bf16[4,32,512]{2,1,0:T(8,128)(2,1)S(1)} collective-permute-done((bf16[4,32,512]{2,1,0:T(8,128)(2,1)S(1)}, bf16[4,32,512]{2,1,0:T(8,128)(2,1)S(1)}, u32[]{:S(2)}, u32[]{:S(2)}) %collective-permute-start.1) | collective-permute-done | bytes 131104 | tf_op jit(solution)/shard_map/ppermute | solution.py:15
  55.5 0.2 add_convert_fusion
  55.8 1.5 %collective-permute-start.2 = (bf16[4,32,512]{2,1,0:T(8,128)(2,1)S(1)}, bf16[4,32,512]{2,1,0:T(8,128)(2,1)S(1)}, u32[]{:S(2)}, u32[]{:S(2)}) collective-permute-start(bf16[4,32,512]{2,1,0:T(8,128)(2,1)S(1)} %add_convert_fusion), channel_id=1, source_target_pairs={{8,0},{16,8},{24,16},{9,1},{17,9},{25,17},{10,2},{18,10},{26,18},{... | collective-permute-start | bytes 393224 | tf_op jit(solution)/shard_map/ppermute | solution.py:15
  57.3 0.0 copy-done.7
  57.3 1.3 %fusion.16 = bf16[4,32,512]{2,1,0:T(8,128)(2,1)S(1)} fusion(bf16[1,1,512,512]{3,2,1,0:T(8,128)(2,1)} %param.15, bf16[1,4,32,512]{3,2,1,0:T(8,128)(2,1)S(1)} %copy-done.7), kind=kOutput, calls=%fused_computation.21 | convolution fusion | flops 67174400 | bytes 786432 | tf_op jit(solution)/shard_map/qtid,ide->qtie/dot_general | solution.py:38
  58.6 0.6 dynamic-slice
  59.9 0.7 dynamic_slice.10
  60.5 2.7 %collective-permute-done.2 = bf16[4,32,512]{2,1,0:T(8,128)(2,1)S(1)} collective-permute-done((bf16[4,32,512]{2,1,0:T(8,128)(2,1)S(1)}, bf16[4,32,512]{2,1,0:T(8,128)(2,1)S(1)}, u32[]{:S(2)}, u32[]{:S(2)}) %collective-permute-start.2) | collective-permute-done | bytes 131104 | tf_op jit(solution)/shard_map/ppermute | solution.py:15
  63.2 0.2 convolution_convert_fusion.2
  63.5 0.0 copy-start.6
  63.5 3.2 %fusion.13 = bf16[4,512,512]{2,1,0:T(8,128)(2,1)} fusion(bf16[4,32,512]{2,1,0:T(8,128)(2,1)S(1)} %bitcast.96, bf16[4,32,512]{2,1,0:T(8,128)(2,1)S(1)} %fusion.16, f32[512,512]{1,0:T(8,128)S(1)} %add_bitcast_fusion, bf16[1,1,512,512]{3,2,1,0:T(8,128)(2,1)S(1)} %copy-done), kind=kOutput, calls=%fused_computation.13 | convolution fusion | flops 1142947840 | bytes 3932160 | tf_op jit(solution)/shard_map/cd,qdf->qcf/dot_general | solution.py:46
  66.7 2.9 %fusion.10 = bf16[4,512,512]{2,1,0:T(8,128)(2,1)S(1)} fusion(bf16[4,512,512]{2,1,0:T(8,128)(2,1)} %fusion.13, bf16[1,1,512,512]{3,2,1,0:T(8,128)(2,1)S(1)} %copy-done.6), kind=kOutput, calls=%fused_computation.12 | convolution fusion | flops 1074790400 | bytes 4718592 | tf_op jit(solution)/shard_map/qcie,ife->qcif/dot_general | solution.py:50
  69.6 3.0 %copy.29 = bf16[4,512,512]{2,0,1:T(4,128)(2,1)} copy(bf16[4,512,512]{2,1,0:T(8,128)(2,1)S(1)} %fusion.10) | data formatting | bytes 4194304 | tf_op jit(solution)/shard_map/while | solution.py:75
  72.5 0.0 all-to-all-done
  72.5 4.3 %reshape.96 = bf16[4096,1,128]{2,1,0:T(2,128)(2,1)S(1)} reshape(bf16[8,2,32768]{2,1,0:T(2,128)(2,1)} %all-to-all-done) | data formatting | bytes 2097152
  76.9 1.1 copy.35
  78.0 1.5 %copy.26 = bf16[1,8,128,512]{3,2,1,0:T(8,128)(2,1)S(1)} copy(bf16[1,8,128,512]{2,3,1,0:T(8,128)(2,1)} %bitcast.94) | data formatting | bytes 2097152 | tf_op jit(solution)/shard_map/all_to_all | solution.py:102
  79.5 0.0 all-gather.2.cloned.1.call-done
  79.5 12.8 %while.10 = (s32[]{:T(128)}, f32[2,8,4]{1,0,2:T(2,128)S(1)}, bf16[2,8,64,512]{3,2,1,0:T(8,128)(2,1)S(1)}, bf16[2,8,64,512]{3,2,1,0:T(8,128)(2,1)}, bf16[4,512,512]{2,0,1:T(4,128)(2,1)}, /*index=5*/s32[]{:T(128)}, s32[]{:T(128)}) while((s32[]{:T(128)}, f32[2,8,4]{1,0,2:T(2,128)S(1)}, bf16[2,8,64,512]{3,2,1,0:T(8,128)(2,1)S(1)}, ...), condition=%wide.region_1.2_spmd, body=%wide.region_0.1_spmd.sunk | while | flops 287309824 | bytes 19924460 | solution.py:75
  79.5 2.5 %convolution_convert_fusion.4 = bf16[8,512,512]{2,1,0:T(8,128)(2,1)S(1)} fusion(bf16[2,8,64,512]{3,2,1,0:T(8,128)(2,1)} %get-tuple-element.111, s32[]{:T(128)} %get-tuple-element.101, bf16[2,8,64,512]{3,2,1,0:T(8,128)(2,1)S(1)} %get-tuple-element.110), kind=kOutput, calls=%fused_computation.2.clone.1 | convolution fusion | flops 270532608 | bytes 5243904 | tf_op jit(solution)/shard_map/while/body/eval_jaxpr/btd,bte->bde/dot_general | solution.py:70
  82.0 3.8 %fusion.47 = f32[8,4,1]{0,1,2:T(4,128)S(1)} fusion(bf16[4,512,512]{2,0,1:T(4,128)(2,1)S(1)} %copy-done.2, bf16[8,512,512]{2,1,0:T(8,128)(2,1)S(1)} %convolution_convert_fusion.4), kind=kOutput, calls=%fused_computation.clone.1 | convolution fusion | flops 16777216 | bytes 6291584 | tf_op jit(solution)/shard_map/while/body/eval_jaxpr/bde,qde->bq/dot_general | solution.py:73
  85.9 2.5 %convolution_convert_fusion.4 = bf16[8,512,512]{2,1,0:T(8,128)(2,1)S(1)} fusion(bf16[2,8,64,512]{3,2,1,0:T(8,128)(2,1)} %get-tuple-element.111, s32[]{:T(128)} %get-tuple-element.101, bf16[2,8,64,512]{3,2,1,0:T(8,128)(2,1)S(1)} %get-tuple-element.110), kind=kOutput, calls=%fused_computation.2.clone.1 | convolution fusion | flops 270532608 | bytes 5243904 | tf_op jit(solution)/shard_map/while/body/eval_jaxpr/btd,bte->bde/dot_general | solution.py:70
  88.4 3.8 %fusion.47 = f32[8,4,1]{0,1,2:T(4,128)S(1)} fusion(bf16[4,512,512]{2,0,1:T(4,128)(2,1)S(1)} %copy-done.2, bf16[8,512,512]{2,1,0:T(8,128)(2,1)S(1)} %convolution_convert_fusion.4), kind=kOutput, calls=%fused_computation.clone.1 | convolution fusion | flops 16777216 | bytes 6291584 | tf_op jit(solution)/shard_map/while/body/eval_jaxpr/bde,qde->bq/dot_general | solution.py:73
  92.3 0.1 reshape.88
  92.4 0.3 fusion.29
  92.6 13.1 %all-reduce = f32[4,16]{0,1:T(8,128)S(1)} all-reduce(f32[4,16]{0,1:T(8,128)S(1)} %fusion.29), channel_id=2, replica_groups=mesh['seg'=4,'blk'=8] {'blk'}, use_global_device_ids=true, to_apply=%region_2.3.clone | all-reduce | flops 64 | bytes 512
  105.7 0.7 compare_convert_fusion
  106.4 11.2 %psum.7 = f32[4,2]{0,1:T(2,128)S(1)} all-reduce(f32[4,2]{0,1:T(2,128)S(1)} %constant_dynamic-slice_fusion), channel_id=1, replica_groups=mesh['seg'=4,'blk'=8] {'seg'}, use_global_device_ids=true, to_apply=%region_3.4 | all-reduce | flops 8 | bytes 64 | tf_op jit(solution)/shard_map/psum | solution.py:111
  117.5 0.6 broadcast_multiply_fusion
  (21 shorter events, 0.2 us)
Async XLA Ops:
  6.5 56.7 %copy-start = (bf16[1,1,512,512]{3,2,1,0:T(8,128)(2,1)S(1)}, bf16[1,1,512,512]{3,2,1,0:T(8,128)(2,1)}, u32[]{:S(2)}) copy-start(bf16[1,1,512,512]{3,2,1,0:T(8,128)(2,1)} %param.16) | copy-start | bytes 1572868
  8.0 38.5 %collective-permute-start = (bf16[4,32,512]{2,1,0:T(8,128)(2,1)S(1)}, bf16[4,32,512]{2,1,0:T(8,128)(2,1)S(1)}, u32[]{:S(2)}, u32[]{:S(2)}) collective-permute-start(bf16[4,32,512]{2,1,0:T(8,128)(2,1)S(1)} %fusion.15), channel_id=1, source_target_pairs={{8,0},{16,8},{24,16},{9,1},{17,9},{25,17},{10,2},{18,10},{26,18},{... | collective-permute-start | bytes 393224 | tf_op jit(solution)/shard_map/ppermute | solution.py:15
  38.2 8.3 %copy-start.5 = (bf16[4,32,512]{2,1,0:T(8,128)(2,1)S(1)}, bf16[4,32,512]{2,1,0:T(8,128)(2,1)}, u32[]{:S(2)}) copy-start(bf16[4,32,512]{2,1,0:T(8,128)(2,1)} %param.21) | copy-start | bytes 393220
  38.2 8.4 %copy-start.1 = (bf16[1,1,512,512]{3,2,1,0:T(8,128)(2,1)S(1)}, bf16[1,1,512,512]{3,2,1,0:T(8,128)(2,1)}, u32[]{:S(2)}) copy-start(bf16[1,1,512,512]{3,2,1,0:T(8,128)(2,1)} %param.18) | copy-start | bytes 1572868
  38.2 8.4 %copy-start.4 = (bf16[1,4,32,512]{3,2,1,0:T(8,128)(2,1)S(1)}, bf16[1,4,32,512]{3,2,1,0:T(8,128)(2,1)}, u32[]{:S(2)}) copy-start(bf16[1,4,32,512]{3,2,1,0:T(8,128)(2,1)} %param.19) | copy-start | bytes 393220
  40.4 7.7 %copy-start.3 = (bf16[1,1,512,512]{3,2,1,0:T(8,128)(2,1)S(1)}, bf16[1,1,512,512]{3,2,1,0:T(8,128)(2,1)}, u32[]{:S(2)}) copy-start(bf16[1,1,512,512]{3,2,1,0:T(8,128)(2,1)} %param.17) | copy-start | bytes 1572868
  40.4 32.1 %all-to-all-start = ((bf16[8,2,32768]{2,1,0:T(2,128)(2,1)}), bf16[8,2,32768]{2,1,0:T(2,128)(2,1)}, u32[]{:S(2)}, u32[]{:S(2)}) async-start(bf16[8,2,32768]{2,1,0:T(2,128)(2,1)} %reshape.95), calls=%async_computation | async-start | bytes 2097152 | tf_op jit(solution)/shard_map/all_to_all | solution.py:102
  45.8 11.5 %copy-start.7 = (bf16[1,4,32,512]{3,2,1,0:T(8,128)(2,1)S(1)}, bf16[1,4,32,512]{3,2,1,0:T(8,128)(2,1)}, u32[]{:S(2)}) copy-start(bf16[1,4,32,512]{3,2,1,0:T(8,128)(2,1)} %param.20) | copy-start | bytes 393220
  45.8 33.7 %all-gather.2.cloned.1.call-start = ((), (), s32[]{:S(2)}) async-start(), calls=%async_computation.1 | async-start | bytes 1179648 | tf_op jit(solution)/shard_map/all_gather | solution.py:105
  46.6 12.0 %copy-start.9 = (u32[32]{0:T(128)S(1)}, u32[32]{0:T(128)}, u32[]{:S(2)}) copy-start(u32[32]{0:T(128)} %constant.56) | copy-start | bytes 388
  46.6 13.3 %copy-start.8 = (s32[8]{0:T(128)S(1)}, s32[8]{0:T(128)}, u32[]{:S(2)}) copy-start(s32[8]{0:T(128)} %param.14) | copy-start | bytes 100
  46.9 8.7 %collective-permute-start.1 = (bf16[4,32,512]{2,1,0:T(8,128)(2,1)S(1)}, bf16[4,32,512]{2,1,0:T(8,128)(2,1)S(1)}, u32[]{:S(2)}, u32[]{:S(2)}) collective-permute-start(bf16[4,32,512]{2,1,0:T(8,128)(2,1)S(1)} %add_convert_fusion.1), channel_id=1, source_target_pairs={{8,0},{16,8},{24,16},{9,1},{17,9},{25,17},{10,2},{18,10},{26,18},{... | collective-permute-start | bytes 393224 | tf_op jit(solution)/shard_map/ppermute | solution.py:15
  55.8 7.4 %collective-permute-start.2 = (bf16[4,32,512]{2,1,0:T(8,128)(2,1)S(1)}, bf16[4,32,512]{2,1,0:T(8,128)(2,1)S(1)}, u32[]{:S(2)}, u32[]{:S(2)}) collective-permute-start(bf16[4,32,512]{2,1,0:T(8,128)(2,1)S(1)} %add_convert_fusion), channel_id=1, source_target_pairs={{8,0},{16,8},{24,16},{9,1},{17,9},{25,17},{10,2},{18,10},{26,18},{... | collective-permute-start | bytes 393224 | tf_op jit(solution)/shard_map/ppermute | solution.py:15
  63.5 3.2 %copy-start.6 = (bf16[1,1,512,512]{3,2,1,0:T(8,128)(2,1)S(1)}, bf16[1,1,512,512]{3,2,1,0:T(8,128)(2,1)}, u32[]{:S(2)}) copy-start(bf16[1,1,512,512]{3,2,1,0:T(8,128)(2,1)} %param.15) | copy-start | bytes 1572868
  79.5 2.5 %copy-start.2 = (bf16[4,512,512]{2,0,1:T(4,128)(2,1)S(1)}, bf16[4,512,512]{2,0,1:T(4,128)(2,1)}, u32[]{:S(2)}) copy-start(bf16[4,512,512]{2,0,1:T(4,128)(2,1)} %get-tuple-element.112) | copy-start | bytes 6291460 | tf_op jit(solution)/shard_map/while
  85.9 2.5 %copy-start.2 = (bf16[4,512,512]{2,0,1:T(4,128)(2,1)S(1)}, bf16[4,512,512]{2,0,1:T(4,128)(2,1)}, u32[]{:S(2)}) copy-start(bf16[4,512,512]{2,0,1:T(4,128)(2,1)} %get-tuple-element.112) | copy-start | bytes 6291460 | tf_op jit(solution)/shard_map/while
Sparse Core Ops, SparseCore 0:
  48.5 26.8 all-gather.1
where the time goes:
time: 126 us; the launch traced here: 125 us
  other arithmetic  24.9 us (20%)
  blocking collectives  24.2 us (19%)
  matrix products  22.4 us (18%)
  local copies, waits for them, and re-layouts  19.1 us (15%)
  between operations  14.3 us (11%)
  waiting for transfers between devices  10.6 us (8%)
  starting transfers between devices  9.43 us (7%)
    unnamed x1, other arithmetic  23.4 us
    unnamed x25, local copies, waits for them, and re-layouts  13.9 us
    unnamed x1, blocking collectives  13.1 us
    psum x1, blocking collectives, body(): mine = lax.psum(mine, 'seg')  11.2 us
    ppermute x3, waiting for transfers between devices, passed_along(): lax.ppermute(value, axis, [(source, source + steps) for source in range(f...  9.91 us
    dot_general x2, matrix products, one_batch(): jnp.einsum('bde,qde->bq', outer_prod, precond, preferred_element_type=jnp...  7.62 us
    all_to_all x1, starting transfers between devices, body(): lax.all_to_all(train_grads, 'blk', split_axis=2, concat_axis=1, tiled=True)  5.33 us
    dot_general x2, matrix products, one_batch(): jnp.einsum('btd,bte->bde', grad_block, act_block, preferred_element_type=...  4.98 us
  transfers between devices with their start and end apart: 5, of which 2 were waited for; matrix products, arithmetic and copies ran while one was open for 40% of the time, Pallas kernels for 0%

commit v1 on v0

--- a/solution.py
+++ b/solution.py
@@ -108,7 +108,8 @@
     placement = (slot_of[:, None] == slot_ids[None, :]).astype(jnp.float32)
     local_scores = jnp.dot(scores_part.T, placement, precision=lax.Precision.HIGHEST)
     mine = lax.psum_scatter(local_scores, "blk", scatter_dimension=1, tiled=True)
-    mine = lax.psum(mine, "seg")
+    parts = lax.all_gather(mine, "seg")
+    mine = jnp.sum(parts, axis=0)
     own_valid = (jnp.arange(SLOTS, dtype=jnp.int32) < counts[blk_index]).astype(jnp.float32)
     return mine * own_valid[None, :]
 

time: 126 us -> 125 us (level)
    psum x1 -> x0, blocking collectives: 11.2 us -> none  [body(): mine = lax.psum(mine, 'seg')]
    all_gather x0 -> x1, blocking collectives: none -> 10.4 us  [body(): parts = lax.all_gather(mine, 'seg')]
  transfers between devices with their start and end apart: 5 -> 5, of which waited for: 2 -> 2; matrix products, arithmetic and copies ran while one was open for 40% -> 41% of each run, Pallas kernels for 0% -> 0%
where the time goes in v1:
time: 125 us; the launch traced here: 124 us
  other arithmetic  24.9 us (20%)
  blocking collectives  23.4 us (19%)
  matrix products  22.4 us (18%)
  local copies, waits for them, and re-layouts  19.1 us (15%)
  between operations  14.3 us (11%)
  waiting for transfers between devices  10.6 us (8%)
  starting transfers between devices  9.43 us (8%)
    unnamed x1, other arithmetic  23.4 us
    unnamed x25, local copies, waits for them, and re-layouts  13.9 us
    unnamed x1, blocking collectives  13.1 us
    all_gather x1, blocking collectives, body(): parts = lax.all_gather(mine, 'seg')  10.4 us
    ppermute x3, waiting for transfers between devices, passed_along(): lax.ppermute(value, axis, [(source, source + steps) for source in range(f...  9.91 us
    dot_general x2, matrix products, one_batch(): jnp.einsum('bde,qde->bq', outer_prod, precond, preferred_element_type=jnp...  7.62 us
    all_to_all x1, starting transfers between devices, body(): lax.all_to_all(train_grads, 'blk', split_axis=2, concat_axis=1, tiled=True)  5.33 us
    dot_general x2, matrix products, one_batch(): jnp.einsum('btd,bte->bde', grad_block, act_block, preferred_element_type=...  4.98 us
  transfers between devices with their start and end apart: 5, of which 2 were waited for; matrix products, arithmetic and copies ran while one was open for 41% of the time, Pallas kernels for 0%

profile of v1, /device:TPU:0, one launch (start us, length us, event | category | flops | bytes accessed | tf_op | source)
XLA Modules:
  0.0 124.2 jit_solution(12554309127313614516)
XLA Ops:
  6.5 0.0 copy-start
  6.5 1.4 %fusion.15 = bf16[4,32,512]{2,1,0:T(8,128)(2,1)S(1)} fusion(bf16[4,32,512]{2,1,0:T(8,128)(2,1)} %param.21, bf16[1,1,512,512]{3,2,1,0:T(8,128)(2,1)} %param.18, bf16[1,4,32,512]{3,2,1,0:T(8,128)(2,1)} %param.19), kind=kOutput, calls=%fused_computation.20 | convolution fusion | flops 67436544 | bytes 917504 | tf_op jit(solution)/shard_map/dot_general | solution.py:20
  8.0 1.3 %collective-permute-start = (bf16[4,32,512]{2,1,0:T(8,128)(2,1)S(1)}, bf16[4,32,512]{2,1,0:T(8,128)(2,1)S(1)}, u32[]{:S(2)}, u32[]{:S(2)}) collective-permute-start(bf16[4,32,512]{2,1,0:T(8,128)(2,1)S(1)} %fusion.15), channel_id=1, source_target_pairs={{8,0},{16,8},{24,16},{9,1},{17,9},{25,17},{10,2},{18,10},{26,18},{... | collective-permute-start | bytes 393224 | tf_op jit(solution)/shard_map/ppermute | solution.py:15
  9.3 5.0 %copy.25 = bf16[1,128,4096]{1,0,2:T(2,128)(2,1)S(1)} copy(bf16[1,128,4096]{2,1,0:T(8,128)(2,1)} %param.13) | data formatting | bytes 2097152 | tf_op args[1]
  14.3 0.5 broadcast.63
  14.8 23.4 %reduce.1 = bf16[4096,128]{1,0:T(8,128)(2,1)} reduce(bf16[4096,1,128]{2,1,0:T(2,128)(2,1)S(1)} %bitcast.94, bf16[]{:T(256)} %broadcast.63), dimensions={1}, to_apply=%bitcast.75.reduce_sub_computation | reduce | bytes 2097154
  38.2 2.2 %reshape.99 = bf16[8,2,32768]{2,1,0:T(2,128)(2,1)} reshape(bf16[4096,128]{1,0:T(8,128)(2,1)} %reduce.1) | data formatting | bytes 2097152
  40.4 5.3 %all-to-all-start = ((bf16[8,2,32768]{2,1,0:T(2,128)(2,1)}), bf16[8,2,32768]{2,1,0:T(2,128)(2,1)}, u32[]{:S(2)}, u32[]{:S(2)}) async-start(bf16[8,2,32768]{2,1,0:T(2,128)(2,1)} %reshape.99), calls=%async_computation | async-start | bytes 2097152 | tf_op jit(solution)/shard_map/all_to_all | solution.py:102
  45.8 0.0 all-gather.4.cloned.1.call-start
  45.8 0.7 all-gather.4.cloned.1.call-update
  46.5 0.0 collective-permute-done
  46.5 0.0 copy-done.5
  46.6 0.0 copy-done.1
  46.6 0.0 copy-start.9
  46.6 0.0 copy-start.8
  46.6 0.2 add_convert_fusion.1
  46.9 1.3 %collective-permute-start.1 = (bf16[4,32,512]{2,1,0:T(8,128)(2,1)S(1)}, bf16[4,32,512]{2,1,0:T(8,128)(2,1)S(1)}, u32[]{:S(2)}, u32[]{:S(2)}) collective-permute-start(bf16[4,32,512]{2,1,0:T(8,128)(2,1)S(1)} %add_convert_fusion.1), channel_id=1, source_target_pairs={{8,0},{16,8},{24,16},{9,1},{17,9},{25,17},{10,2},{18,10},{26,18},{... | collective-permute-start | bytes 393224 | tf_op jit(solution)/shard_map/ppermute | solution.py:15
  48.2 0.0 copy-done.3
  48.2 0.1 add_bitcast_fusion
  48.3 7.2 %collective-permute-done.1 = bf16[4,32,512]{2,1,0:T(8,128)(2,1)S(1)} collective-permute-done((bf16[4,32,512]{2,1,0:T(8,128)(2,1)S(1)}, bf16[4,32,512]{2,1,0:T(8,128)(2,1)S(1)}, u32[]{:S(2)}, u32[]{:S(2)}) %collective-permute-start.1) | collective-permute-done | bytes 131104 | tf_op jit(solution)/shard_map/ppermute | solution.py:15
  55.5 0.2 add_convert_fusion
  55.8 1.5 %collective-permute-start.2 = (bf16[4,32,512]{2,1,0:T(8,128)(2,1)S(1)}, bf16[4,32,512]{2,1,0:T(8,128)(2,1)S(1)}, u32[]{:S(2)}, u32[]{:S(2)}) collective-permute-start(bf16[4,32,512]{2,1,0:T(8,128)(2,1)S(1)} %add_convert_fusion), channel_id=1, source_target_pairs={{8,0},{16,8},{24,16},{9,1},{17,9},{25,17},{10,2},{18,10},{26,18},{... | collective-permute-start | bytes 393224 | tf_op jit(solution)/shard_map/ppermute | solution.py:15
  57.3 0.0 copy-done.7
  57.3 1.3 %fusion.16 = bf16[4,32,512]{2,1,0:T(8,128)(2,1)S(1)} fusion(bf16[1,1,512,512]{3,2,1,0:T(8,128)(2,1)} %param.15, bf16[1,4,32,512]{3,2,1,0:T(8,128)(2,1)S(1)} %copy-done.7), kind=kOutput, calls=%fused_computation.21 | convolution fusion | flops 67174400 | bytes 786432 | tf_op jit(solution)/shard_map/qtid,ide->qtie/dot_general | solution.py:38
  58.6 0.6 dynamic-slice
  59.9 0.7 dynamic_slice.10
  60.5 2.7 %collective-permute-done.2 = bf16[4,32,512]{2,1,0:T(8,128)(2,1)S(1)} collective-permute-done((bf16[4,32,512]{2,1,0:T(8,128)(2,1)S(1)}, bf16[4,32,512]{2,1,0:T(8,128)(2,1)S(1)}, u32[]{:S(2)}, u32[]{:S(2)}) %collective-permute-start.2) | collective-permute-done | bytes 131104 | tf_op jit(solution)/shard_map/ppermute | solution.py:15
  63.2 0.2 convolution_convert_fusion.2
  63.5 0.0 copy-start.6
  63.5 3.2 %fusion.13 = bf16[4,512,512]{2,1,0:T(8,128)(2,1)} fusion(bf16[4,32,512]{2,1,0:T(8,128)(2,1)S(1)} %bitcast.98, bf16[4,32,512]{2,1,0:T(8,128)(2,1)S(1)} %fusion.16, f32[512,512]{1,0:T(8,128)S(1)} %add_bitcast_fusion, bf16[1,1,512,512]{3,2,1,0:T(8,128)(2,1)S(1)} %copy-done), kind=kOutput, calls=%fused_computation.13 | convolution fusion | flops 1142947840 | bytes 3932160 | tf_op jit(solution)/shard_map/cd,qdf->qcf/dot_general | solution.py:46
  66.7 2.9 %fusion.10 = bf16[4,512,512]{2,1,0:T(8,128)(2,1)S(1)} fusion(bf16[4,512,512]{2,1,0:T(8,128)(2,1)} %fusion.13, bf16[1,1,512,512]{3,2,1,0:T(8,128)(2,1)S(1)} %copy-done.6), kind=kOutput, calls=%fused_computation.12 | convolution fusion | flops 1074790400 | bytes 4718592 | tf_op jit(solution)/shard_map/qcie,ife->qcif/dot_general | solution.py:50
  69.6 3.0 %copy.29 = bf16[4,512,512]{2,0,1:T(4,128)(2,1)} copy(bf16[4,512,512]{2,1,0:T(8,128)(2,1)S(1)} %fusion.10) | data formatting | bytes 4194304 | tf_op jit(solution)/shard_map/while | solution.py:75
  72.5 0.0 all-to-all-done
  72.5 4.3 %reshape.100 = bf16[4096,1,128]{2,1,0:T(2,128)(2,1)S(1)} reshape(bf16[8,2,32768]{2,1,0:T(2,128)(2,1)} %all-to-all-done) | data formatting | bytes 2097152
  76.9 1.1 copy.35
  78.0 1.5 %copy.26 = bf16[1,8,128,512]{3,2,1,0:T(8,128)(2,1)S(1)} copy(bf16[1,8,128,512]{2,3,1,0:T(8,128)(2,1)} %bitcast.96) | data formatting | bytes 2097152 | tf_op jit(solution)/shard_map/all_to_all | solution.py:102
  79.5 0.0 all-gather.4.cloned.1.call-done
  79.5 12.8 %while.10 = (s32[]{:T(128)}, f32[2,8,4]{1,0,2:T(2,128)S(1)}, bf16[2,8,64,512]{3,2,1,0:T(8,128)(2,1)S(1)}, bf16[2,8,64,512]{3,2,1,0:T(8,128)(2,1)}, bf16[4,512,512]{2,0,1:T(4,128)(2,1)}, /*index=5*/s32[]{:T(128)}, s32[]{:T(128)}) while((s32[]{:T(128)}, f32[2,8,4]{1,0,2:T(2,128)S(1)}, bf16[2,8,64,512]{3,2,1,0:T(8,128)(2,1)S(1)}, ...), condition=%wide.region_1.2_spmd, body=%wide.region_0.1_spmd.sunk | while | flops 287309824 | bytes 19924460 | solution.py:75
  79.5 2.5 %convolution_convert_fusion.4 = bf16[8,512,512]{2,1,0:T(8,128)(2,1)S(1)} fusion(bf16[2,8,64,512]{3,2,1,0:T(8,128)(2,1)} %get-tuple-element.111, s32[]{:T(128)} %get-tuple-element.101, bf16[2,8,64,512]{3,2,1,0:T(8,128)(2,1)S(1)} %get-tuple-element.110), kind=kOutput, calls=%fused_computation.2.clone.1 | convolution fusion | flops 270532608 | bytes 5243904 | tf_op jit(solution)/shard_map/while/body/eval_jaxpr/btd,bte->bde/dot_general | solution.py:70
  82.0 3.8 %fusion.47 = f32[8,4,1]{0,1,2:T(4,128)S(1)} fusion(bf16[4,512,512]{2,0,1:T(4,128)(2,1)S(1)} %copy-done.2, bf16[8,512,512]{2,1,0:T(8,128)(2,1)S(1)} %convolution_convert_fusion.4), kind=kOutput, calls=%fused_computation.clone.1 | convolution fusion | flops 16777216 | bytes 6291584 | tf_op jit(solution)/shard_map/while/body/eval_jaxpr/bde,qde->bq/dot_general | solution.py:73
  85.9 2.5 %convolution_convert_fusion.4 = bf16[8,512,512]{2,1,0:T(8,128)(2,1)S(1)} fusion(bf16[2,8,64,512]{3,2,1,0:T(8,128)(2,1)} %get-tuple-element.111, s32[]{:T(128)} %get-tuple-element.101, bf16[2,8,64,512]{3,2,1,0:T(8,128)(2,1)S(1)} %get-tuple-element.110), kind=kOutput, calls=%fused_computation.2.clone.1 | convolution fusion | flops 270532608 | bytes 5243904 | tf_op jit(solution)/shard_map/while/body/eval_jaxpr/btd,bte->bde/dot_general | solution.py:70
  88.4 3.8 %fusion.47 = f32[8,4,1]{0,1,2:T(4,128)S(1)} fusion(bf16[4,512,512]{2,0,1:T(4,128)(2,1)S(1)} %copy-done.2, bf16[8,512,512]{2,1,0:T(8,128)(2,1)S(1)} %convolution_convert_fusion.4), kind=kOutput, calls=%fused_computation.clone.1 | convolution fusion | flops 16777216 | bytes 6291584 | tf_op jit(solution)/shard_map/while/body/eval_jaxpr/bde,qde->bq/dot_general | solution.py:73
  92.3 0.1 reshape.88
  92.4 0.3 fusion.29
  92.6 13.1 %all-reduce = f32[4,16]{0,1:T(8,128)S(1)} all-reduce(f32[4,16]{0,1:T(8,128)S(1)} %fusion.29), channel_id=3, replica_groups=mesh['seg'=4,'blk'=8] {'blk'}, use_global_device_ids=true, to_apply=%region_2.3.clone | all-reduce | flops 64 | bytes 512
  105.7 0.7 compare_convert_fusion
  106.4 10.4 %all-gather.1 = f32[4,4,2]{1,2,0:T(2,128)S(1)} all-gather(f32[1,4,2]{1,2,0:T(2,128)S(1)} %dynamic-slice_bitcast_fusion), channel_id=2, replica_groups=mesh['seg'=4,'blk'=8] {'seg'}, dimensions={0}, use_global_device_ids=true | all-gather | bytes 160 | tf_op jit(solution)/shard_map/all_gather | solution.py:111
  116.8 0.6 broadcast_multiply_fusion
  (22 shorter events, 0.2 us)
Async XLA Ops:
  6.5 56.7 %copy-start = (bf16[1,1,512,512]{3,2,1,0:T(8,128)(2,1)S(1)}, bf16[1,1,512,512]{3,2,1,0:T(8,128)(2,1)}, u32[]{:S(2)}) copy-start(bf16[1,1,512,512]{3,2,1,0:T(8,128)(2,1)} %param.16) | copy-start | bytes 1572868
  8.0 38.5 %collective-permute-start = (bf16[4,32,512]{2,1,0:T(8,128)(2,1)S(1)}, bf16[4,32,512]{2,1,0:T(8,128)(2,1)S(1)}, u32[]{:S(2)}, u32[]{:S(2)}) collective-permute-start(bf16[4,32,512]{2,1,0:T(8,128)(2,1)S(1)} %fusion.15), channel_id=1, source_target_pairs={{8,0},{16,8},{24,16},{9,1},{17,9},{25,17},{10,2},{18,10},{26,18},{... | collective-permute-start | bytes 393224 | tf_op jit(solution)/shard_map/ppermute | solution.py:15
  38.2 8.3 %copy-start.5 = (bf16[4,32,512]{2,1,0:T(8,128)(2,1)S(1)}, bf16[4,32,512]{2,1,0:T(8,128)(2,1)}, u32[]{:S(2)}) copy-start(bf16[4,32,512]{2,1,0:T(8,128)(2,1)} %param.21) | copy-start | bytes 393220
  38.2 8.4 %copy-start.1 = (bf16[1,1,512,512]{3,2,1,0:T(8,128)(2,1)S(1)}, bf16[1,1,512,512]{3,2,1,0:T(8,128)(2,1)}, u32[]{:S(2)}) copy-start(bf16[1,1,512,512]{3,2,1,0:T(8,128)(2,1)} %param.18) | copy-start | bytes 1572868
  38.2 8.4 %copy-start.4 = (bf16[1,4,32,512]{3,2,1,0:T(8,128)(2,1)S(1)}, bf16[1,4,32,512]{3,2,1,0:T(8,128)(2,1)}, u32[]{:S(2)}) copy-start(bf16[1,4,32,512]{3,2,1,0:T(8,128)(2,1)} %param.19) | copy-start | bytes 393220
  40.4 7.7 %copy-start.3 = (bf16[1,1,512,512]{3,2,1,0:T(8,128)(2,1)S(1)}, bf16[1,1,512,512]{3,2,1,0:T(8,128)(2,1)}, u32[]{:S(2)}) copy-start(bf16[1,1,512,512]{3,2,1,0:T(8,128)(2,1)} %param.17) | copy-start | bytes 1572868
  40.4 32.1 %all-to-all-start = ((bf16[8,2,32768]{2,1,0:T(2,128)(2,1)}), bf16[8,2,32768]{2,1,0:T(2,128)(2,1)}, u32[]{:S(2)}, u32[]{:S(2)}) async-start(bf16[8,2,32768]{2,1,0:T(2,128)(2,1)} %reshape.99), calls=%async_computation | async-start | bytes 2097152 | tf_op jit(solution)/shard_map/all_to_all | solution.py:102
  45.8 11.5 %copy-start.7 = (bf16[1,4,32,512]{3,2,1,0:T(8,128)(2,1)S(1)}, bf16[1,4,32,512]{3,2,1,0:T(8,128)(2,1)}, u32[]{:S(2)}) copy-start(bf16[1,4,32,512]{3,2,1,0:T(8,128)(2,1)} %param.20) | copy-start | bytes 393220
  45.8 33.7 %all-gather.4.cloned.1.call-start = ((), (), s32[]{:S(2)}) async-start(), calls=%async_computation.1 | async-start | bytes 1179648 | tf_op jit(solution)/shard_map/all_gather | solution.py:105
  46.6 12.0 %copy-start.9 = (u32[32]{0:T(128)S(1)}, u32[32]{0:T(128)}, u32[]{:S(2)}) copy-start(u32[32]{0:T(128)} %constant.57) | copy-start | bytes 388
  46.6 13.3 %copy-start.8 = (s32[8]{0:T(128)S(1)}, s32[8]{0:T(128)}, u32[]{:S(2)}) copy-start(s32[8]{0:T(128)} %param.14) | copy-start | bytes 100
  46.9 8.7 %collective-permute-start.1 = (bf16[4,32,512]{2,1,0:T(8,128)(2,1)S(1)}, bf16[4,32,512]{2,1,0:T(8,128)(2,1)S(1)}, u32[]{:S(2)}, u32[]{:S(2)}) collective-permute-start(bf16[4,32,512]{2,1,0:T(8,128)(2,1)S(1)} %add_convert_fusion.1), channel_id=1, source_target_pairs={{8,0},{16,8},{24,16},{9,1},{17,9},{25,17},{10,2},{18,10},{26,18},{... | collective-permute-start | bytes 393224 | tf_op jit(solution)/shard_map/ppermute | solution.py:15
  55.8 7.4 %collective-permute-start.2 = (bf16[4,32,512]{2,1,0:T(8,128)(2,1)S(1)}, bf16[4,32,512]{2,1,0:T(8,128)(2,1)S(1)}, u32[]{:S(2)}, u32[]{:S(2)}) collective-permute-start(bf16[4,32,512]{2,1,0:T(8,128)(2,1)S(1)} %add_convert_fusion), channel_id=1, source_target_pairs={{8,0},{16,8},{24,16},{9,1},{17,9},{25,17},{10,2},{18,10},{26,18},{... | collective-permute-start | bytes 393224 | tf_op jit(solution)/shard_map/ppermute | solution.py:15
  63.5 3.2 %copy-start.6 = (bf16[1,1,512,512]{3,2,1,0:T(8,128)(2,1)S(1)}, bf16[1,1,512,512]{3,2,1,0:T(8,128)(2,1)}, u32[]{:S(2)}) copy-start(bf16[1,1,512,512]{3,2,1,0:T(8,128)(2,1)} %param.15) | copy-start | bytes 1572868
  79.5 2.5 %copy-start.2 = (bf16[4,512,512]{2,0,1:T(4,128)(2,1)S(1)}, bf16[4,512,512]{2,0,1:T(4,128)(2,1)}, u32[]{:S(2)}) copy-start(bf16[4,512,512]{2,0,1:T(4,128)(2,1)} %get-tuple-element.112) | copy-start | bytes 6291460 | tf_op jit(solution)/shard_map/while
  85.9 2.5 %copy-start.2 = (bf16[4,512,512]{2,0,1:T(4,128)(2,1)S(1)}, bf16[4,512,512]{2,0,1:T(4,128)(2,1)}, u32[]{:S(2)}) copy-start(bf16[4,512,512]{2,0,1:T(4,128)(2,1)} %get-tuple-element.112) | copy-start | bytes 6291460 | tf_op jit(solution)/shard_map/while
Sparse Core Ops, SparseCore 0:
  48.5 26.8 all-gather.3
